TPU v7x, 256 devices: a whole 4x4x8 slice. The times are simulated.
256 devices in a mesh: chan: 32 (over x, y, core), wide: 8 (over z).
Axes of the slice: x: 4, y: 4, z: 8, core: 2. Of those that a mesh axis runs over, the one named last changes fastest.
Arguments:
- conc_now: float32 [8, 64, 64, 1024], P(None, 'chan', None, 'wide'), may hold values from 0.01 to 1
- conc_prev: float32 [8, 64, 64, 1024], P(None, 'chan', None, 'wide'), may hold values from 0.1 to 1
- phi_prev: float32 [64, 64, 1024], P('chan', None, 'wide'), may hold values from -3 to 3
- owner: int32 [64, 64, 1024], P('chan', None, 'wide'), may hold values from 0 to 2048, as said below
- partner: int32 [2048], replicated, may hold values from 0 to 2047, each once
- valence: int32 [8], replicated, may hold values from -2 to 2
- diffusivity: float32 [8], replicated, may hold values from 0.2 to 1
Outputs:
- conc_next: float32 [8, 64, 64, 1024], P(None, 'chan', None, 'wide')
- potential: float32 [64, 64, 1024], P('chan', None, 'wide')
Inputs may be any that keep to these rules, and one draw needn't show every extreme that they name: `owner`: the value 2048 marks a cell of no junction. The cells of one junction lie within one block of 2 cells along the length and 128 along the width, aligned with the grid. Some junctions own no cell. `partner`: every junction appears once.
All inputs are finite; a program needn't handle non-finite values.
Results may differ from a plain program's by a relative error of at most 0.00029.
Values sent between devices are 32-bit elements; how exact they have to be, the bound alone decides.
A program may use at most 128 MiB of HBM per device.

v0:
```python
import math
import jax
import jax.numpy as jnp
from jax import lax
from jax.sharding import PartitionSpec as P

SWEEPS = 4
time_step = 0.5
coupling = 2.0
charge_scale = 0.05
conduct_ref = 1.5
highest = lax.Precision.HIGHEST


def with_halo(cells, sides, width):
    for axis, dim in sides:
        count = lax.axis_size(axis)
        ends = count - 1
        head = lax.slice_in_dim(cells, 0, width, axis=dim)
        tail = lax.slice_in_dim(cells, cells.shape[dim] - width, cells.shape[dim], axis=dim)
        cells = jnp.concatenate(
            [
                lax.ppermute(tail, axis, [(i, (i + 1) % count) for i in range(ends)]),
                cells,
                lax.ppermute(head, axis, [((i + 1) % count, i) for i in range(ends)]),
            ],
            axis=dim,
        )
    return cells


def sine_table(length):
    index = jnp.arange(length).astype(jnp.float32) + 1.0
    return math.sqrt(2.0 / (length + 1.0)) * jnp.sin(
        math.pi * index[:, None] * index[None, :] / (length + 1.0)
    )


def eigen_values(length):
    index = jnp.arange(length).astype(jnp.float32) + 1.0
    return 2.0 - 2.0 * jnp.cos(math.pi * index / (length + 1.0))


def conductivity(concs, valence, diffusivity):
    charge_sq = (valence * valence).astype(jnp.float32)
    weights = charge_sq * diffusivity / jnp.sum((charge_sq + 1.0) * diffusivity)
    return 1.0 + jnp.sum(weights[:, None, None, None] * concs * concs, axis=0)


def neighbours(padded, depth_mode):
    middle = padded[..., 1:-1, :, 1:-1]
    widths = [(0, 0)] * (padded.ndim - 3) + [(0, 0), (1, 1), (0, 0)]
    depth_padded = jnp.pad(middle, widths, mode=depth_mode)
    return [
        padded[..., :-2, :, 1:-1],
        padded[..., 2:, :, 1:-1],
        depth_padded[..., :-2, :],
        depth_padded[..., 2:, :],
        padded[..., 1:-1, :, :-2],
        padded[..., 1:-1, :, 2:],
    ]


def rim_replace(padded, lower_x, upper_x, lower_y, upper_y):
    low_plane = jnp.where(lower_x, padded[..., 1:2, :, :], padded[..., 0:1, :, :])
    high_plane = jnp.where(upper_x, padded[..., -2:-1, :, :], padded[..., -1:, :, :])
    padded = jnp.concatenate([low_plane, padded[..., 1:-1, :, :], high_plane], axis=-3)
    low_plane = jnp.where(lower_y, padded[..., 1:2], padded[..., 0:1])
    high_plane = jnp.where(upper_y, padded[..., -2:-1], padded[..., -1:])
    return jnp.concatenate([low_plane, padded[..., 1:-1], high_plane], axis=-1)


def halo_potential(potential_field):
    return with_halo(potential_field, (("chan", 0), ("wide", 2)), 1)


def per_device(conc_now, conc_prev, phi_prev, owner, partner, valence, diffusivity):
    species_all, cells_x, depth_all, cells_y = conc_now.shape
    chan_total = lax.axis_size("chan")
    wide_total = lax.axis_size("wide")
    chan_place = lax.axis_index("chan")
    wide_place = lax.axis_index("wide")
    length_all = cells_x * chan_total
    width_all = cells_y * wide_total
    depth_piece = depth_all // wide_total
    width_piece = width_all // chan_total
    junction_total = partner.shape[0]
    lower_x = chan_place == 0
    upper_x = chan_place == chan_total - 1
    lower_y = wide_place == 0
    upper_y = wide_place == wide_total - 1
    table_x = sine_table(length_all)
    table_z = sine_table(depth_all)
    table_y = sine_table(width_all)
    eigen_x = eigen_values(length_all)
    eigen_y = eigen_values(width_all)
    eigen_z = lax.dynamic_slice_in_dim(
        eigen_values(depth_all), wide_place * depth_piece, depth_piece
    )
    charge_weights = valence.astype(jnp.float32)[:, None, None, None]
    drift = (valence.astype(jnp.float32) * diffusivity)[:, None, None, None]
    spread = diffusivity[:, None, None, None]
    owners = jnp.minimum(owner.reshape(-1), junction_total)
    cell_counts = jax.ops.segment_sum(
        jnp.ones(owners.shape, jnp.float32), owners, num_segments=junction_total + 1
    )
    concs = conc_now
    potential_field = phi_prev
    conc_raw = with_halo(concs, (("chan", 1), ("wide", 3)), 1)
    sigma_local = conductivity(concs, valence, diffusivity)
    sigma_padded = with_halo(sigma_local, (("chan", 0), ("wide", 2)), 1)
    charge = charge_scale * jnp.sum(charge_weights * concs, axis=0)
    for sweep_step in range(SWEEPS):
        phi_padded = halo_potential(potential_field)
        apply_phi_near_all = neighbours(phi_padded, "constant")
        sigma_near_all = neighbours(sigma_padded, "constant")
        sigma_mid = sigma_padded[1:-1, :, 1:-1]
        applied = jnp.zeros_like(potential_field)
        for apply_phi_near, sigma_near in zip(apply_phi_near_all, sigma_near_all):
            applied = applied + 0.5 * (sigma_mid + sigma_near) * (potential_field - apply_phi_near)
        spectrum = jnp.einsum("az,xzy->xay", table_z, charge - applied, precision=highest)
        spectrum = lax.all_to_all(spectrum, "wide", split_axis=1, concat_axis=2, tiled=True)
        across = jnp.einsum("xzy,yb->xzb", spectrum, table_y, precision=highest)
        lined = lax.all_to_all(across, "chan", split_axis=2, concat_axis=0, tiled=True)
        lined = jnp.einsum("ax,xzy->azy", table_x, lined, precision=highest)
        eigen_part = lax.dynamic_slice_in_dim(eigen_y, chan_place * width_piece, width_piece)
        lined = lined / (
            conduct_ref
            * (eigen_x[:, None, None] + eigen_z[None, :, None] + eigen_part[None, None, :])
        )
        lined = jnp.einsum("ax,xzy->azy", table_x, lined, precision=highest)
        across = lax.all_to_all(lined, "chan", split_axis=0, concat_axis=2, tiled=True)
        spectrum = jnp.einsum("xzy,yb->xzb", across, table_y, precision=highest)
        spectrum = lax.all_to_all(spectrum, "wide", split_axis=2, concat_axis=1, tiled=True)
        potential_field = potential_field + jnp.einsum(
            "az,xzy->xay", table_z, spectrum, precision=highest
        )
    cell_rows = concs.reshape(species_all, -1).T
    junction_sums = jax.ops.segment_sum(cell_rows, owners, num_segments=junction_total + 1)
    junction_sums, total_counts = lax.psum((junction_sums, cell_counts), ("chan", "wide"))
    means = junction_sums / jnp.maximum(total_counts, 1.0)[:, None]
    own_means = means[:junction_total]
    table = coupling * (own_means[partner] - own_means)
    table = jnp.concatenate([table, jnp.zeros((1, species_all), jnp.float32)], axis=0)
    source = table[owners].T.reshape(concs.shape)
    conc_fixed = rim_replace(conc_raw, lower_x, upper_x, lower_y, upper_y)
    phi_fixed = rim_replace(halo_potential(potential_field), lower_x, upper_x, lower_y, upper_y)
    conc_near_all = neighbours(conc_fixed, "edge")
    phi_near_all = neighbours(phi_fixed, "edge")
    diagonal_part = jnp.zeros_like(concs) + 1.5 / time_step
    gathered_terms = (4.0 * conc_now - conc_prev) / (2.0 * time_step) + source
    for conc_near, phi_near in zip(conc_near_all, phi_near_all):
        velocity = drift * (potential_field - phi_near)[None]
        diagonal_part = diagonal_part + spread + jnp.maximum(velocity, 0.0)
        gathered_terms = gathered_terms + (spread + jnp.maximum(-velocity, 0.0)) * conc_near
    concs = gathered_terms / diagonal_part
    return (concs, potential_field)


def solution(mesh):
    return jax.shard_map(
        per_device,
        mesh=mesh,
        in_specs=(
            P(None, "chan", None, "wide"),
            P(None, "chan", None, "wide"),
            P("chan", None, "wide"),
            P("chan", None, "wide"),
            P(),
            P(),
            P(),
        ),
        out_specs=(P(None, "chan", None, "wide"), P("chan", None, "wide")),
        check_vma=False,
    )
```

profile of v0, /device:TPU:34, one launch (start us, length us, event | category | flops | bytes accessed | tf_op | source)
XLA Modules:
  0.0 887.7 jit_solution(6742743469902880809)
XLA Ops:
  15.3 4.1 collective-permute-start.3
  29.9 5.4 collective-permute-done
  35.4 3.8 collective-permute-start.4
  43.3 3.9 collective-permute-start.5
  51.3 11.0 %all-to-all-start = ((f32[2,64,128]{2,0,1:T(2,128)}), f32[2,64,128]{2,0,1:T(2,128)S(1)}, u32[]{:S(2)}, u32[]{:S(2)}) async-start(f32[2,64,128]{2,0,1:T(2,128)} %copy.85), calls=%async_computation | async-start | bytes 131072 | tf_op jit(solution)/shard_map/all_to_all | solution.py:122
  62.4 6.8 all-to-all-done
  69.2 16.9 %fusion.14 = f32[2,8,1024]{2,1,0:T(8,128)S(1)} fusion(f32[1024]{0:T(1024)S(1)} %get-tuple-element.64, f32[1024]{0:T(1024)S(1)} %get-tuple-element.65, f32[2,8,8,128]{3,0,2,1:T(2,128)S(1)} %bitcast.241), kind=kOutput, calls=%fused_computation.18 | convolution fusion | flops 204472320 | bytes 139264 | tf_op jit(solution)/shard_map/xzy,yb->xzb/dot_general | solution.py:123
  88.8 5.0 all-to-all-start.1
  93.9 6.2 all-to-all-done.1
  105.0 10.9 %all_to_all.288 = f32[32,1,512]{2,1,0:T(1,128)S(1)} all-to-all(f32[32,1,512]{2,1,0:T(1,128)S(1)} %reshape.173), channel_id=1, replica_groups=mesh['chan'=32,'wide'=8] {'chan'}, dimensions={0} | all-to-all | bytes 131072 | tf_op jit(solution)/shard_map/all_to_all | solution.py:132
  117.0 16.6 %fusion.12 = f32[2,8,1024]{2,1,0:T(8,128)S(1)} fusion(f32[2,8,1024]{2,1,0:T(8,128)S(1)} %all_to_all.219, f32[1024]{0:T(1024)S(1)} %get-tuple-element.64, f32[1024]{0:T(1024)S(1)} %get-tuple-element.65), kind=kOutput, calls=%fused_computation.16 | convolution fusion | flops 204472320 | bytes 139264 | tf_op jit(solution)/shard_map/xzy,yb->xzb/dot_general | solution.py:133
  135.8 10.8 %all_to_all.289 = f32[8,1,2048]{2,1,0:T(1,128)S(1)} all-to-all(f32[8,1,2048]{2,1,0:T(1,128)S(1)} %reshape.175), channel_id=1, replica_groups=mesh['chan'=32,'wide'=8] {'wide'}, dimensions={0} | all-to-all | bytes 131072 | tf_op jit(solution)/shard_map/all_to_all | solution.py:134
  154.2 5.4 collective-permute-done.8
  170.4 12.4 %all_to_all.290 = f32[2,64,128]{2,0,1:T(2,128)S(1)} all-to-all(f32[2,64,128]{2,0,1:T(2,128)S(1)} %copy.94), channel_id=1, replica_groups=mesh['chan'=32,'wide'=8] {'wide'}, dimensions={1} | all-to-all | bytes 131072 | tf_op jit(solution)/shard_map/all_to_all | solution.py:122
  182.8 16.6 %fusion.10 = f32[2,8,1024]{2,1,0:T(8,128)S(1)} fusion(f32[1024]{0:T(1024)S(1)} %get-tuple-element.64, f32[1024]{0:T(1024)S(1)} %get-tuple-element.65, f32[2,8,8,128]{3,0,2,1:T(2,128)S(1)} %bitcast.244), kind=kOutput, calls=%fused_computation.14 | convolution fusion | flops 204472320 | bytes 139264 | tf_op jit(solution)/shard_map/xzy,yb->xzb/dot_general | solution.py:123
  202.2 4.1 all-to-all-start.5
  206.3 4.3 collective-permute-start.25
  217.6 5.0 all-to-all-start.6
  223.5 4.6 copy.125
  228.2 110.4 %scatter_custom_fusion = f32[2049,8]{1,0:T(8,128)} fusion(s32[16384]{0:T(1024)S(1)} %bitcast.237, f32[16384,8]{1,0:T(8,128)} %bitcast.196, f32[]{:T(128)} %constant.28.clone.1), kind=kCustom, calls=%fused_computation.84 | custom fusion | flops 131072 | bytes 66080 | tf_op jit(solution)/shard_map/scatter-add | solution.py:139
  339.7 16.8 %fusion.8 = f32[2,8,1024]{2,1,0:T(8,128)S(1)} fusion(f32[2,8,1024]{2,1,0:T(8,128)S(1)} %all_to_all.235, f32[1024]{0:T(1024)S(1)} %copy-done.21, f32[1024]{0:T(1024)S(1)} %copy-done.25), kind=kOutput, calls=%fused_computation.12 | convolution fusion | flops 204472320 | bytes 139264 | tf_op jit(solution)/shard_map/xzy,yb->xzb/dot_general | solution.py:133
  359.3 3.9 all-to-all-start.7
  363.3 7.0 all-to-all-done.7
  378.4 109.7 %scatter_custom_fusion.1 = f32[2049]{0:T(1024)S(1)} fusion(s32[16384]{0:T(1024)S(1)} %bitcast.239, f32[16384]{0:T(1024)S(1)} %broadcast.172, f32[]{:T(128)} %constant.28.clone.1), kind=kCustom, calls=%fused_computation.420 | custom fusion | flops 16384 | bytes 8200 | tf_op jit(solution)/shard_map/scatter-add | solution.py:104
  494.1 79.7 %psum.15 = f32[2049]{0:T(1024)S(1)} all-reduce(f32[2049]{0:T(1024)S(1)} %scatter_custom_fusion.1), channel_id=1, replica_groups=mesh['chan'=32,'wide'=8] {'chan','wide'}, use_global_device_ids=true, to_apply=%region_3.0 | all-reduce | flops 2049 | bytes 16392 | tf_op jit(solution)/shard_map/psum | solution.py:140
  575.0 3.6 all-to-all-start.8
  579.3 6.3 all-to-all-done.8
  585.6 17.3 %fusion.6 = f32[2,8,1024]{2,1,0:T(8,128)S(1)} fusion(f32[1024]{0:T(1024)} %copy-done.20, f32[1024]{0:T(1024)} %copy-done.24, f32[2,8,8,128]{3,0,2,1:T(2,128)S(1)} %bitcast.243), kind=kOutput, calls=%fused_computation.10 | convolution fusion | flops 204472320 | bytes 139264 | tf_op jit(solution)/shard_map/xzy,yb->xzb/dot_general | solution.py:123
  605.6 5.3 all-to-all-start.9
  611.0 6.4 all-to-all-done.9
  622.4 5.4 all-to-all-start.10
  627.8 5.9 all-to-all-done.10
  634.9 16.6 %fusion.4 = f32[2,8,1024]{2,1,0:T(8,128)S(1)} fusion(f32[2,8,1024]{2,1,0:T(8,128)S(1)} %all_to_all.251, f32[1024]{0:T(1024)S(1)} %copy-done.22, f32[1024]{0:T(1024)S(1)} %copy-done.26), kind=kOutput, calls=%fused_computation.8 | convolution fusion | flops 204472320 | bytes 139264 | tf_op jit(solution)/shard_map/xzy,yb->xzb/dot_general | solution.py:133
  654.2 4.7 all-to-all-start.11
  660.5 7.6 gather_fusion
  677.6 4.4 collective-permute-done.16
  698.5 7.5 all-to-all-start.12
  708.1 54.5 %gather_fusion.1 = f32[16384,8]{1,0:T(8,128)} fusion(f32[2049,8]{1,0:T(8,128)S(1)} %concatenate.143, s32[16384]{0:T(1024)S(1)} %copy-done.13), kind=kCustom, calls=%fused_computation.1 | custom fusion | bytes 1114112 | tf_op jit(solution)/shard_map/gather | solution.py:145
  762.6 6.1 copy.126
  771.5 16.8 %fusion.2 = f32[2,8,1024]{2,1,0:T(8,128)S(1)} fusion(f32[1024]{0:T(1024)S(1)} %copy-done.23, f32[1024]{0:T(1024)S(1)} %copy-done.27, f32[2,8,8,128]{3,0,2,1:T(2,128)S(1)} %bitcast.242), kind=kOutput, calls=%fused_computation.6 | convolution fusion | flops 204472320 | bytes 139264 | tf_op jit(solution)/shard_map/xzy,yb->xzb/dot_general | solution.py:123
  791.0 4.1 all-to-all-start.13
  797.6 3.9 all-to-all-done.13
  806.4 5.2 all-to-all-start.14
  812.8 5.0 all-to-all-done.14
  819.0 16.6 %fusion = f32[2,8,1024]{2,1,0:T(8,128)S(1)} fusion(f32[2,8,1024]{2,1,0:T(8,128)S(1)} %all_to_all.267, f32[1024]{0:T(1024)S(1)} %copy-done.23, f32[1024]{0:T(1024)S(1)} %copy-done.27), kind=kOutput, calls=%fused_computation.4 | convolution fusion | flops 204472320 | bytes 139264 | tf_op jit(solution)/shard_map/xzy,yb->xzb/dot_general | solution.py:133
  838.4 7.2 all-to-all-start.15
  846.9 5.5 all-to-all-done.15
  863.1 4.2 collective-permute-done.20
  (277 shorter events, 170.4 us)
Async XLA Ops:
  9.0 15.3 %collective-permute-start.24 = (f32[8,1,64,128]{3,2,1,0:T(8,128)S(1)}, f32[8,1,64,128]{3,2,1,0:T(8,128)S(1)}, u32[]{:S(2)}, u32[]{:S(2)}) collective-permute-start(f32[8,1,64,128]{3,2,1,0:T(8,128)S(1)} %get-tuple-element.16), channel_id=1, source_target_pairs={{0,8},{8,16},{16,24},{24,32},{32,40},{40,48},{48,56},{56,64},{64,7... | collective-permute-start | bytes 786440 | tf_op jit(solution)/shard_map/ppermute | solution.py:23
  11.7 11.7 %collective-permute-start.1 = (f32[1,64,128]{2,1,0:T(8,128)S(1)}, f32[1,64,128]{2,1,0:T(8,128)S(1)}, u32[]{:S(2)}, u32[]{:S(2)}) collective-permute-start(f32[1,64,128]{2,1,0:T(8,128)S(1)} %get-tuple-element.56), channel_id=1, source_target_pairs={{0,8},{8,16},{16,24},{24,32},{32,40},{40,48},{48,56},{56,64},{64,7... | collective-permute-start | bytes 98312 | tf_op jit(solution)/shard_map/ppermute | solution.py:23
  15.3 14.6 %collective-permute-start.3 = (f32[1,64,128]{2,1,0:T(8,128)S(1)}, f32[1,64,128]{2,1,0:T(8,128)S(1)}, u32[]{:S(2)}, u32[]{:S(2)}) collective-permute-start(f32[1,64,128]{2,1,0:T(8,128)S(1)} %get-tuple-element.55), channel_id=1, source_target_pairs={{8,0},{16,8},{24,16},{32,24},{40,32},{48,40},{56,48},{64,56},{72,6... | collective-permute-start | bytes 98312 | tf_op jit(solution)/shard_map/ppermute | solution.py:25
  25.5 548.4 %copy-start.6 = (f32[2,64,128]{2,1,0:T(8,128)}, f32[2,64,128]{2,1,0:T(8,128)S(1)}, u32[]{:S(2)}) copy-start(f32[2,64,128]{2,1,0:T(8,128)S(1)} %get-tuple-element.4) | copy-start | bytes 196612
  25.5 4.4 collective-permute-start.2
  27.9 7.3 collective-permute-start
  29.9 140.0 %copy-start.7 = (f32[1,64,128]{2,1,0:T(8,128)}, f32[1,64,128]{2,1,0:T(8,128)S(1)}, u32[]{:S(2)}) copy-start(f32[1,64,128]{2,1,0:T(8,128)S(1)} %collective-permute-done.2) | copy-start | bytes 98308
  35.3 134.6 %copy-start.9 = (f32[1,64,128]{2,1,0:T(8,128)}, f32[1,64,128]{2,1,0:T(8,128)S(1)}, u32[]{:S(2)}) copy-start(f32[1,64,128]{2,1,0:T(8,128)S(1)} %collective-permute-done) | copy-start | bytes 98308
  35.4 11.8 %collective-permute-start.4 = (f32[4,64,1]{2,1,0:T(8,128)S(1)}, f32[4,64,1]{2,1,0:T(8,128)S(1)}, u32[]{:S(2)}, u32[]{:S(2)}) collective-permute-start(f32[4,64,1]{2,1,0:T(8,128)S(1)} %get-tuple-element.37), channel_id=1, source_target_pairs={{0,1},{1,2},{2,3},{3,4},{4,5},{5,6},{6,7},{8,9},{9,10},{10,11},{11... | collective-permute-start | bytes 3080 | tf_op jit(solution)/shard_map/ppermute | solution.py:23
  39.2 8.0 collective-permute-start.6
  41.4 6.9 collective-permute-start.7
  43.3 6.9 collective-permute-start.5
  51.3 17.9 %all-to-all-start = ((f32[2,64,128]{2,0,1:T(2,128)}), f32[2,64,128]{2,0,1:T(2,128)S(1)}, u32[]{:S(2)}, u32[]{:S(2)}) async-start(f32[2,64,128]{2,0,1:T(2,128)} %copy.85), calls=%async_computation | async-start | bytes 131072 | tf_op jit(solution)/shard_map/all_to_all | solution.py:122
  62.3 120.5 %copy-start.24 = (f32[1024]{0:T(1024)}, f32[1024]{0:T(1024)S(1)}, u32[]{:S(2)}) copy-start(f32[1024]{0:T(1024)S(1)} %get-tuple-element.65) | copy-start | bytes 12292
  88.8 11.3 %all-to-all-start.1 = ((f32[32,1,512]{2,1,0:T(1,128)}), f32[32,1,512]{2,1,0:T(1,128)S(1)}, u32[]{:S(2)}, u32[]{:S(2)}) async-start(f32[32,1,512]{2,1,0:T(1,128)} %reshape.171), calls=%async_computation.1 | async-start | bytes 131072 | tf_op jit(solution)/shard_map/all_to_all | solution.py:124
  149.7 4.5 collective-permute-start.9
  152.3 7.3 collective-permute-start.8
  159.7 6.9 collective-permute-start.11
  163.0 6.9 collective-permute-start.10
  202.2 10.4 %all-to-all-start.5 = ((f32[32,1,512]{2,1,0:T(1,128)}), f32[32,1,512]{2,1,0:T(1,128)S(1)}, u32[]{:S(2)}, u32[]{:S(2)}) async-start(f32[32,1,512]{2,1,0:T(1,128)} %reshape.177), calls=%async_computation.5 | async-start | bytes 131072 | tf_op jit(solution)/shard_map/all_to_all | solution.py:124
  206.3 470.3 %collective-permute-start.25 = (f32[8,1,64,128]{3,2,1,0:T(8,128)}, f32[8,1,64,128]{3,2,1,0:T(8,128)}, u32[]{:S(2)}, u32[]{:S(2)}) collective-permute-start(f32[8,1,64,128]{3,2,1,0:T(8,128)} %get-tuple-element.15), channel_id=1, source_target_pairs={{8,0},{16,8},{24,16},{32,24},{40,32},{48,40},{56,48},{64,56},{72,6... | collective-permute-start | bytes 786440 | tf_op jit(solution)/shard_map/ppermute | solution.py:25
  217.6 121.0 %all-to-all-start.6 = ((f32[32,1,512]{2,1,0:T(1,128)}), f32[32,1,512]{2,1,0:T(1,128)S(1)}, u32[]{:S(2)}, u32[]{:S(2)}) async-start(f32[32,1,512]{2,1,0:T(1,128)} %reshape.179), calls=%async_computation.6 | async-start | bytes 131072 | tf_op jit(solution)/shard_map/all_to_all | solution.py:132
  222.6 436.3 %all-reduce.8.cloned.1.call-start = ((), (), s32[]{:S(2)}) async-start(), calls=%async_computation.16 | async-start | bytes 2105344 | tf_op jit(solution)/shard_map/psum | solution.py:140
  356.5 217.3 %copy-start.8 = (f32[1,64,128]{2,1,0:T(8,128)S(1)}, f32[1,64,128]{2,1,0:T(8,128)}, u32[]{:S(2)}) copy-start(f32[1,64,128]{2,1,0:T(8,128)} %copy-done.7) | copy-start | bytes 98308
  356.5 217.3 %copy-start.10 = (f32[1,64,128]{2,1,0:T(8,128)S(1)}, f32[1,64,128]{2,1,0:T(8,128)}, u32[]{:S(2)}) copy-start(f32[1,64,128]{2,1,0:T(8,128)} %copy-done.9) | copy-start | bytes 98308
  359.3 10.9 %all-to-all-start.7 = ((f32[8,1,2048]{2,1,0:T(1,128)}), f32[8,1,2048]{2,1,0:T(1,128)S(1)}, u32[]{:S(2)}, u32[]{:S(2)}) async-start(f32[8,1,2048]{2,1,0:T(1,128)} %reshape.181), calls=%async_computation.7 | async-start | bytes 131072 | tf_op jit(solution)/shard_map/all_to_all | solution.py:134
  373.4 114.7 %collective-permute-start.13 = (f32[1,64,128]{2,1,0:T(8,128)S(1)}, f32[1,64,128]{2,1,0:T(8,128)S(1)}, u32[]{:S(2)}, u32[]{:S(2)}) collective-permute-start(f32[1,64,128]{2,1,0:T(8,128)S(1)} %get-tuple-element.50), channel_id=1, source_target_pairs={{8,0},{16,8},{24,16},{32,24},{40,32},{48,40},{56,48},{64,56},{72,6... | collective-permute-start | bytes 98312 | tf_op jit(solution)/shard_map/ppermute | solution.py:25
  375.9 112.3 %collective-permute-start.12 = (f32[1,64,128]{2,1,0:T(8,128)S(1)}, f32[1,64,128]{2,1,0:T(8,128)S(1)}, u32[]{:S(2)}, u32[]{:S(2)}) collective-permute-start(f32[1,64,128]{2,1,0:T(8,128)S(1)} %get-tuple-element.49), channel_id=1, source_target_pairs={{0,8},{8,16},{16,24},{24,32},{32,40},{40,48},{48,56},{56,64},{64,7... | collective-permute-start | bytes 98312 | tf_op jit(solution)/shard_map/ppermute | solution.py:23
  488.3 85.6 %collective-permute-start.15 = (f32[4,64,1]{2,1,0:T(8,128)S(1)}, f32[4,64,1]{2,1,0:T(8,128)S(1)}, u32[]{:S(2)}, u32[]{:S(2)}) collective-permute-start(f32[4,64,1]{2,1,0:T(8,128)S(1)} %get-tuple-element.30), channel_id=1, source_target_pairs={{1,0},{2,1},{3,2},{4,3},{5,4},{6,5},{7,6},{9,8},{10,9},{11,10},{12... | collective-permute-start | bytes 3080 | tf_op jit(solution)/shard_map/ppermute | solution.py:25
  490.6 83.2 %collective-permute-start.14 = (f32[4,64,1]{2,1,0:T(8,128)S(1)}, f32[4,64,1]{2,1,0:T(8,128)S(1)}, u32[]{:S(2)}, u32[]{:S(2)}) collective-permute-start(f32[4,64,1]{2,1,0:T(8,128)S(1)} %get-tuple-element.29), channel_id=1, source_target_pairs={{0,1},{1,2},{2,3},{3,4},{4,5},{5,6},{6,7},{8,9},{9,10},{10,11},{11... | collective-permute-start | bytes 3080 | tf_op jit(solution)/shard_map/ppermute | solution.py:23
  575.0 10.5 %all-to-all-start.8 = ((f32[2,64,128]{2,0,1:T(2,128)}), f32[2,64,128]{2,0,1:T(2,128)S(1)}, u32[]{:S(2)}, u32[]{:S(2)}) async-start(f32[2,64,128]{2,0,1:T(2,128)} %copy.103), calls=%async_computation.8 | async-start | bytes 131072 | tf_op jit(solution)/shard_map/all_to_all | solution.py:122
  605.6 11.8 %all-to-all-start.9 = ((f32[32,1,512]{2,1,0:T(1,128)}), f32[32,1,512]{2,1,0:T(1,128)S(1)}, u32[]{:S(2)}, u32[]{:S(2)}) async-start(f32[32,1,512]{2,1,0:T(1,128)} %reshape.183), calls=%async_computation.9 | async-start | bytes 131072 | tf_op jit(solution)/shard_map/all_to_all | solution.py:124
  622.4 11.4 %all-to-all-start.10 = ((f32[32,1,512]{2,1,0:T(1,128)}), f32[32,1,512]{2,1,0:T(1,128)S(1)}, u32[]{:S(2)}, u32[]{:S(2)}) async-start(f32[32,1,512]{2,1,0:T(1,128)} %reshape.185), calls=%async_computation.10 | async-start | bytes 131072 | tf_op jit(solution)/shard_map/all_to_all | solution.py:132
  654.2 13.9 %all-to-all-start.11 = ((f32[8,1,2048]{2,1,0:T(1,128)}), f32[8,1,2048]{2,1,0:T(1,128)S(1)}, u32[]{:S(2)}, u32[]{:S(2)}) async-start(f32[8,1,2048]{2,1,0:T(1,128)} %reshape.187), calls=%async_computation.11 | async-start | bytes 131072 | tf_op jit(solution)/shard_map/all_to_all | solution.py:134
  671.3 6.3 collective-permute-start.17
  674.7 7.3 collective-permute-start.16
  682.8 13.6 %collective-permute-start.19 = (f32[4,64,1]{2,1,0:T(8,128)}, f32[4,64,1]{2,1,0:T(8,128)}, u32[]{:S(2)}, u32[]{:S(2)}) collective-permute-start(f32[4,64,1]{2,1,0:T(8,128)} %get-tuple-element.28), channel_id=1, source_target_pairs={{1,0},{2,1},{3,2},{4,3},{5,4},{6,5},{7,6},{9,8},{10,9},{11,10},{12... | collective-permute-start | bytes 3080 | tf_op jit(solution)/shard_map/ppermute | solution.py:25
  685.2 11.2 %collective-permute-start.18 = (f32[4,64,1]{2,1,0:T(8,128)}, f32[4,64,1]{2,1,0:T(8,128)}, u32[]{:S(2)}, u32[]{:S(2)}) collective-permute-start(f32[4,64,1]{2,1,0:T(8,128)} %get-tuple-element.27), channel_id=1, source_target_pairs={{0,1},{1,2},{2,3},{3,4},{4,5},{5,6},{6,7},{8,9},{9,10},{10,11},{11... | collective-permute-start | bytes 3080 | tf_op jit(solution)/shard_map/ppermute | solution.py:23
  690.0 78.6 %collective-permute-start.27 = (f32[8,4,64,1]{2,0,3,1:T(8,128)}, f32[8,4,64,1]{2,0,3,1:T(8,128)S(1)}, u32[]{:S(2)}, u32[]{:S(2)}) collective-permute-start(f32[8,4,64,1]{2,0,3,1:T(8,128)} %copy.122), channel_id=1, source_target_pairs={{1,0},{2,1},{3,2},{4,3},{5,4},{6,5},{7,6},{9,8},{10,9},{11,10},{12... | collective-permute-start | bytes 24584 | tf_op jit(solution)/shard_map/ppermute | solution.py:25
  693.5 76.6 %collective-permute-start.26 = (f32[8,4,64,1]{2,0,3,1:T(8,128)S(1)}, f32[8,4,64,1]{2,0,3,1:T(8,128)S(1)}, u32[]{:S(2)}, u32[]{:S(2)}) collective-permute-start(f32[8,4,64,1]{2,0,3,1:T(8,128)S(1)} %copy.121), channel_id=1, source_target_pairs={{0,1},{1,2},{2,3},{3,4},{4,5},{5,6},{6,7},{8,9},{9,10},{10,11},{11... | collective-permute-start | bytes 24584 | tf_op jit(solution)/shard_map/ppermute | solution.py:23
  698.5 72.9 %all-to-all-start.12 = ((f32[2,64,128]{2,0,1:T(2,128)}), f32[2,64,128]{2,0,1:T(2,128)S(1)}, u32[]{:S(2)}, u32[]{:S(2)}) async-start(f32[2,64,128]{2,0,1:T(2,128)} %copy.112), calls=%async_computation.12 | async-start | bytes 131072 | tf_op jit(solution)/shard_map/all_to_all | solution.py:122
  791.0 10.5 %all-to-all-start.13 = ((f32[32,1,512]{2,1,0:T(1,128)}), f32[32,1,512]{2,1,0:T(1,128)S(1)}, u32[]{:S(2)}, u32[]{:S(2)}) async-start(f32[32,1,512]{2,1,0:T(1,128)} %reshape.189), calls=%async_computation.13 | async-start | bytes 131072 | tf_op jit(solution)/shard_map/all_to_all | solution.py:124
  806.4 11.4 %all-to-all-start.14 = ((f32[32,1,512]{2,1,0:T(1,128)}), f32[32,1,512]{2,1,0:T(1,128)S(1)}, u32[]{:S(2)}, u32[]{:S(2)}) async-start(f32[32,1,512]{2,1,0:T(1,128)} %reshape.191), calls=%async_computation.14 | async-start | bytes 131072 | tf_op jit(solution)/shard_map/all_to_all | solution.py:132
  838.4 14.1 %all-to-all-start.15 = ((f32[8,1,2048]{2,1,0:T(1,128)}), f32[8,1,2048]{2,1,0:T(1,128)S(1)}, u32[]{:S(2)}, u32[]{:S(2)}) async-start(f32[8,1,2048]{2,1,0:T(1,128)} %reshape.193), calls=%async_computation.15 | async-start | bytes 131072 | tf_op jit(solution)/shard_map/all_to_all | solution.py:134
  857.7 5.4 collective-permute-start.21
  859.9 7.3 collective-permute-start.20
  867.4 6.9 collective-permute-start.23
  870.8 6.9 collective-permute-start.22
  (25 other events, 763.5 us)
Sparse Core Ops, SparseCore 0:
  338.7 255.6 all-reduce.7
where the time goes:
time: 900 us; the launch traced here: 888 us
  other arithmetic  249 us (28%)
  starting transfers between devices  150 us (17%)
  matrix products  142 us (16%)
  local copies, waits for them, and re-layouts  132 us (15%)
  blocking collectives  114 us (13%)
  waiting for transfers between devices  86 us (10%)
  between operations  16 us (2%)
    scatter-add x1, other arithmetic, per_device(): jax.ops.segment_sum(cell_rows, owners, num_segments=junction_total + 1)  110 us
    scatter-add x1, other arithmetic, per_device(): jax.ops.segment_sum(jnp.ones(owners.shape, jnp.float32), owners, num_segm...  110 us
    psum x1, blocking collectives, per_device(): lax.psum((junction_sums, cell_counts), ('chan', 'wide'))  79.7 us
    dot_general x4, matrix products, per_device(): across = jnp.einsum('xzy,yb->xzb', spectrum, table_y, precision=highest)  67.5 us
    dot_general x4, matrix products, per_device(): spectrum = jnp.einsum('xzy,yb->xzb', across, table_y, precision=highest)  66.6 us
    gather x1, local copies, waits for them, and re-layouts, per_device(): source = table[owners].T.reshape(concs.shape)  54.5 us
    ppermute x14, starting transfers between devices, with_halo(): lax.ppermute(head, axis, [((i + 1) % count, i) for i in range(ends)])  39.7 us
    ppermute x14, starting transfers between devices, with_halo(): lax.ppermute(tail, axis, [(i, (i + 1) % count) for i in range(ends)])  37.9 us
  transfers between devices with their start and end apart: 42, of which 20 were waited for; matrix products, arithmetic and copies ran while one was open for 45% of the time, Pallas kernels for 0%

commit v1 on v0

--- a/solution.py
+++ b/solution.py
@@ -137,7 +137,7 @@
         )
     cell_rows = concs.reshape(species_all, -1).T
     junction_sums = jax.ops.segment_sum(cell_rows, owners, num_segments=junction_total + 1)
-    junction_sums, total_counts = lax.psum((junction_sums, cell_counts), ("chan", "wide"))
+    junction_sums, total_counts = lax.psum(lax.psum((junction_sums, cell_counts), "chan"), "wide")
     means = junction_sums / jnp.maximum(total_counts, 1.0)[:, None]
     own_means = means[:junction_total]
     table = coupling * (own_means[partner] - own_means)

time: 900 us -> 1020 us (1.13)
  blocking collectives: 114 us -> 177 us
  waiting for transfers between devices: 86 us -> 124 us
  starting transfers between devices: 150 us -> 170 us
    psum x1 -> x2, blocking collectives: 79.7 us -> 132 us  [the longest x1 104 us: per_device(): lax.psum((junction_sums, cell_counts), 'chan')]
    psum x1 -> x2, waiting for transfers between devices: 0.01 us -> 47 us  [the longest x1 46.9 us: per_device(): lax.psum(lax.psum((junction_sums, cell_counts), 'chan'), 'wide')]
    all_to_all x4 -> x3, starting transfers between devices: 18.6 us -> 32.1 us  [per_device(): lax.all_to_all(across, 'chan', split_axis=2, concat_axis=0, tiled=True)]
    all_to_all x0 -> x1, blocking collectives: none -> 10.2 us  [per_device(): lax.all_to_all(across, 'chan', split_axis=2, concat_axis=0, tiled=True)]
    unnamed x89 -> x91, local copies, waits for them, and re-layouts: 34.9 us -> 34.3 us
  transfers between devices with their start and end apart: 42 -> 42, of which waited for: 20 -> 21; matrix products, arithmetic and copies ran while one was open for 45% -> 39% of each run, Pallas kernels for 0% -> 0%
where the time goes in v1:
time: 1020 us; the launch traced here: 1010 us
  other arithmetic  248 us (24%)
  blocking collectives  177 us (17%)
  starting transfers between devices  170 us (17%)
  matrix products  142 us (14%)
  local copies, waits for them, and re-layouts  131 us (13%)
  waiting for transfers between devices  124 us (12%)
  between operations  16 us (2%)
    scatter-add x1, other arithmetic, per_device(): jax.ops.segment_sum(cell_rows, owners, num_segments=junction_total + 1)  110 us
    scatter-add x1, other arithmetic, per_device(): jax.ops.segment_sum(jnp.ones(owners.shape, jnp.float32), owners, num_segm...  110 us
    psum x1, blocking collectives, per_device(): lax.psum((junction_sums, cell_counts), 'chan')  104 us
    dot_general x4, matrix products, per_device(): across = jnp.einsum('xzy,yb->xzb', spectrum, table_y, precision=highest)  67.5 us
    dot_general x4, matrix products, per_device(): spectrum = jnp.einsum('xzy,yb->xzb', across, table_y, precision=highest)  66.6 us
    gather x1, local copies, waits for them, and re-layouts, per_device(): source = table[owners].T.reshape(concs.shape)  54.5 us
    psum x1, waiting for transfers between devices, per_device(): lax.psum(lax.psum((junction_sums, cell_counts), 'chan'), 'wide')  46.9 us
    ppermute x14, starting transfers between devices, with_halo(): lax.ppermute(tail, axis, [(i, (i + 1) % count) for i in range(ends)])  38.6 us
  transfers between devices with their start and end apart: 42, of which 21 were waited for; matrix products, arithmetic and copies ran while one was open for 39% of the time, Pallas kernels for 0%

profile of v1, /device:TPU:34, one launch (start us, length us, event | category | flops | bytes accessed | tf_op | source)
XLA Modules:
  0.0 1007.5 jit_solution(16215715711538498263)
XLA Ops:
  15.3 4.1 collective-permute-start.3
  29.9 5.4 collective-permute-done
  43.3 3.9 collective-permute-start.5
  51.3 11.0 %all-to-all-start = ((f32[2,64,128]{2,0,1:T(2,128)}), f32[2,64,128]{2,0,1:T(2,128)S(1)}, u32[]{:S(2)}, u32[]{:S(2)}) async-start(f32[2,64,128]{2,0,1:T(2,128)} %copy.85), calls=%async_computation | async-start | bytes 131072 | tf_op jit(solution)/shard_map/all_to_all | solution.py:122
  62.4 6.8 all-to-all-done
  69.2 16.6 %fusion.14 = f32[2,8,1024]{2,1,0:T(8,128)S(1)} fusion(f32[1024]{0:T(1024)S(1)} %get-tuple-element.64, f32[1024]{0:T(1024)S(1)} %get-tuple-element.65, f32[2,8,8,128]{3,0,2,1:T(2,128)S(1)} %bitcast.241), kind=kOutput, calls=%fused_computation.18 | convolution fusion | flops 204472320 | bytes 139264 | tf_op jit(solution)/shard_map/xzy,yb->xzb/dot_general | solution.py:123
  88.6 5.0 all-to-all-start.1
  93.7 6.2 all-to-all-done.1
  104.8 10.9 %all_to_all.288 = f32[32,1,512]{2,1,0:T(1,128)S(1)} all-to-all(f32[32,1,512]{2,1,0:T(1,128)S(1)} %reshape.173), channel_id=1, replica_groups=mesh['chan'=32,'wide'=8] {'chan'}, dimensions={0} | all-to-all | bytes 131072 | tf_op jit(solution)/shard_map/all_to_all | solution.py:132
  116.8 16.6 %fusion.12 = f32[2,8,1024]{2,1,0:T(8,128)S(1)} fusion(f32[2,8,1024]{2,1,0:T(8,128)S(1)} %all_to_all.219, f32[1024]{0:T(1024)S(1)} %get-tuple-element.64, f32[1024]{0:T(1024)S(1)} %get-tuple-element.65), kind=kOutput, calls=%fused_computation.16 | convolution fusion | flops 204472320 | bytes 139264 | tf_op jit(solution)/shard_map/xzy,yb->xzb/dot_general | solution.py:133
  135.5 10.8 %all_to_all.289 = f32[8,1,2048]{2,1,0:T(1,128)S(1)} all-to-all(f32[8,1,2048]{2,1,0:T(1,128)S(1)} %reshape.175), channel_id=1, replica_groups=mesh['chan'=32,'wide'=8] {'wide'}, dimensions={0} | all-to-all | bytes 131072 | tf_op jit(solution)/shard_map/all_to_all | solution.py:134
  153.9 5.4 collective-permute-done.8
  170.1 12.4 %all_to_all.290 = f32[2,64,128]{2,0,1:T(2,128)S(1)} all-to-all(f32[2,64,128]{2,0,1:T(2,128)S(1)} %copy.94), channel_id=1, replica_groups=mesh['chan'=32,'wide'=8] {'wide'}, dimensions={1} | all-to-all | bytes 131072 | tf_op jit(solution)/shard_map/all_to_all | solution.py:122
  182.6 16.8 %fusion.10 = f32[2,8,1024]{2,1,0:T(8,128)S(1)} fusion(f32[1024]{0:T(1024)S(1)} %get-tuple-element.64, f32[1024]{0:T(1024)S(1)} %get-tuple-element.65, f32[2,8,8,128]{3,0,2,1:T(2,128)S(1)} %bitcast.244), kind=kOutput, calls=%fused_computation.14 | convolution fusion | flops 204472320 | bytes 139264 | tf_op jit(solution)/shard_map/xzy,yb->xzb/dot_general | solution.py:123
  201.5 10.2 %all_to_all.291 = f32[32,1,512]{2,1,0:T(1,128)S(1)} all-to-all(f32[32,1,512]{2,1,0:T(1,128)S(1)} %reshape.177), channel_id=1, replica_groups=mesh['chan'=32,'wide'=8] {'chan'}, dimensions={0} | all-to-all | bytes 131072 | tf_op jit(solution)/shard_map/all_to_all | solution.py:124
  216.7 5.0 all-to-all-start.6
  221.7 4.3 collective-permute-start.25
  226.0 4.8 copy.125
  232.0 16.8 %fusion.8 = f32[2,8,1024]{2,1,0:T(8,128)S(1)} fusion(f32[2,8,1024]{2,1,0:T(8,128)S(1)} %all_to_all.235, f32[1024]{0:T(1024)S(1)} %copy-done.22, f32[1024]{0:T(1024)S(1)} %copy-done.26), kind=kOutput, calls=%fused_computation.12 | convolution fusion | flops 204472320 | bytes 139264 | tf_op jit(solution)/shard_map/xzy,yb->xzb/dot_general | solution.py:133
  251.6 4.7 all-to-all-start.7
  256.4 110.2 %scatter_custom_fusion = f32[2049,8]{1,0:T(8,128)} fusion(s32[16384]{0:T(1024)S(1)} %bitcast.237, f32[16384,8]{1,0:T(8,128)} %bitcast.196, f32[]{:T(128)} %constant.28.clone.1), kind=kCustom, calls=%fused_computation.84 | custom fusion | flops 131072 | bytes 66080 | tf_op jit(solution)/shard_map/scatter-add | solution.py:139
  374.2 4.8 collective-permute-done.12
  381.1 3.9 collective-permute-start.14
  389.1 9.3 all-to-all-start.8
  399.0 109.7 %scatter_custom_fusion.1 = f32[2049]{0:T(1024)S(1)} fusion(s32[16384]{0:T(1024)S(1)} %bitcast.239, f32[16384]{0:T(1024)S(1)} %broadcast.172, f32[]{:T(128)} %constant.28.clone.1), kind=kCustom, calls=%fused_computation.420 | custom fusion | flops 16384 | bytes 8200 | tf_op jit(solution)/shard_map/scatter-add | solution.py:104
  508.8 104.4 %psum.30 = f32[2049]{0:T(1024)S(1)} all-reduce(f32[2049]{0:T(1024)S(1)} %scatter_custom_fusion.1), channel_id=1, replica_groups=mesh['chan'=32,'wide'=8] {'chan'}, use_global_device_ids=true, to_apply=%region_4.5 | all-reduce | flops 2049 | bytes 16392 | tf_op jit(solution)/shard_map/psum | solution.py:140
  613.2 28.0 %psum.31 = f32[2049]{0:T(1024)S(1)} all-reduce(f32[2049]{0:T(1024)S(1)} %psum.30), channel_id=1, replica_groups=mesh['chan'=32,'wide'=8] {'wide'}, use_global_device_ids=true, to_apply=%region_5.6 | all-reduce | flops 2049 | bytes 16392 | tf_op jit(solution)/shard_map/psum | solution.py:140
  641.2 17.3 %fusion.6 = f32[2,8,1024]{2,1,0:T(8,128)S(1)} fusion(f32[1024]{0:T(1024)} %copy-done.21, f32[1024]{0:T(1024)} %copy-done.25, f32[2,8,8,128]{3,0,2,1:T(2,128)S(1)} %bitcast.243), kind=kOutput, calls=%fused_computation.10 | convolution fusion | flops 204472320 | bytes 139264 | tf_op jit(solution)/shard_map/xzy,yb->xzb/dot_general | solution.py:123
  661.3 21.8 %all-to-all-start.9 = ((f32[32,1,512]{2,1,0:T(1,128)}), f32[32,1,512]{2,1,0:T(1,128)S(1)}, u32[]{:S(2)}, u32[]{:S(2)}) async-start(f32[32,1,512]{2,1,0:T(1,128)} %reshape.183), calls=%async_computation.9 | async-start | bytes 131072 | tf_op jit(solution)/shard_map/all_to_all | solution.py:124
  683.1 6.4 all-to-all-done.9
  694.4 5.0 all-to-all-start.10
  700.1 5.6 all-to-all-done.10
  707.0 16.6 %fusion.4 = f32[2,8,1024]{2,1,0:T(8,128)S(1)} fusion(f32[2,8,1024]{2,1,0:T(8,128)S(1)} %all_to_all.251, f32[1024]{0:T(1024)S(1)} %copy-done.23, f32[1024]{0:T(1024)S(1)} %copy-done.27), kind=kOutput, calls=%fused_computation.8 | convolution fusion | flops 204472320 | bytes 139264 | tf_op jit(solution)/shard_map/xzy,yb->xzb/dot_general | solution.py:133
  726.3 6.2 all-to-all-start.11
  732.5 46.9 %all-reduce.11.cloned.1.call-done = f32[2049,8]{1,0:T(8,128)} async-done(((f32[2049,8]{1,0:T(8,128)}), f32[2049,8]{1,0:T(8,128)}) %all-reduce.11.cloned.1.call-update) | async-done | bytes 65584 | tf_op jit(solution)/shard_map/psum | solution.py:140
  781.0 7.6 gather_fusion
  797.2 3.9 collective-permute-done.16
  817.6 7.1 all-to-all-start.12
  826.7 54.5 %gather_fusion.1 = f32[16384,8]{1,0:T(8,128)} fusion(f32[2049,8]{1,0:T(8,128)S(1)} %concatenate.143, s32[16384]{0:T(1024)S(1)} %copy-done.13), kind=kCustom, calls=%fused_computation.1 | custom fusion | bytes 1114112 | tf_op jit(solution)/shard_map/gather | solution.py:145
  881.2 6.1 copy.126
  890.1 16.8 %fusion.2 = f32[2,8,1024]{2,1,0:T(8,128)S(1)} fusion(f32[1024]{0:T(1024)S(1)} %copy-done.24, f32[1024]{0:T(1024)S(1)} %copy-done.28, f32[2,8,8,128]{3,0,2,1:T(2,128)S(1)} %bitcast.242), kind=kOutput, calls=%fused_computation.6 | convolution fusion | flops 204472320 | bytes 139264 | tf_op jit(solution)/shard_map/xzy,yb->xzb/dot_general | solution.py:123
  909.6 5.3 all-to-all-start.13
  926.2 5.2 all-to-all-start.14
  932.6 5.0 all-to-all-done.14
  938.8 16.6 %fusion = f32[2,8,1024]{2,1,0:T(8,128)S(1)} fusion(f32[2,8,1024]{2,1,0:T(8,128)S(1)} %all_to_all.267, f32[1024]{0:T(1024)S(1)} %copy-done.24, f32[1024]{0:T(1024)S(1)} %copy-done.28), kind=kOutput, calls=%fused_computation.4 | convolution fusion | flops 204472320 | bytes 139264 | tf_op jit(solution)/shard_map/xzy,yb->xzb/dot_general | solution.py:133
  958.1 7.2 all-to-all-start.15
  966.7 5.5 all-to-all-done.15
  982.9 4.2 collective-permute-done.20
  (282 shorter events, 172.6 us)
Async XLA Ops:
  9.0 15.3 %collective-permute-start.24 = (f32[8,1,64,128]{3,2,1,0:T(8,128)S(1)}, f32[8,1,64,128]{3,2,1,0:T(8,128)S(1)}, u32[]{:S(2)}, u32[]{:S(2)}) collective-permute-start(f32[8,1,64,128]{3,2,1,0:T(8,128)S(1)} %get-tuple-element.16), channel_id=1, source_target_pairs={{0,8},{8,16},{16,24},{24,32},{32,40},{40,48},{48,56},{56,64},{64,7... | collective-permute-start | bytes 786440 | tf_op jit(solution)/shard_map/ppermute | solution.py:23
  11.7 11.7 %collective-permute-start.1 = (f32[1,64,128]{2,1,0:T(8,128)S(1)}, f32[1,64,128]{2,1,0:T(8,128)S(1)}, u32[]{:S(2)}, u32[]{:S(2)}) collective-permute-start(f32[1,64,128]{2,1,0:T(8,128)S(1)} %get-tuple-element.56), channel_id=1, source_target_pairs={{0,8},{8,16},{16,24},{24,32},{32,40},{40,48},{48,56},{56,64},{64,7... | collective-permute-start | bytes 98312 | tf_op jit(solution)/shard_map/ppermute | solution.py:23
  15.3 14.6 %collective-permute-start.3 = (f32[1,64,128]{2,1,0:T(8,128)S(1)}, f32[1,64,128]{2,1,0:T(8,128)S(1)}, u32[]{:S(2)}, u32[]{:S(2)}) collective-permute-start(f32[1,64,128]{2,1,0:T(8,128)S(1)} %get-tuple-element.55), channel_id=1, source_target_pairs={{8,0},{16,8},{24,16},{32,24},{40,32},{48,40},{56,48},{64,56},{72,6... | collective-permute-start | bytes 98312 | tf_op jit(solution)/shard_map/ppermute | solution.py:25
  25.5 362.5 %copy-start.6 = (f32[2,64,128]{2,1,0:T(8,128)}, f32[2,64,128]{2,1,0:T(8,128)S(1)}, u32[]{:S(2)}) copy-start(f32[2,64,128]{2,1,0:T(8,128)S(1)} %get-tuple-element.4) | copy-start | bytes 196612
  25.5 4.4 collective-permute-start.2
  27.9 7.3 collective-permute-start
  29.9 139.7 %copy-start.7 = (f32[1,64,128]{2,1,0:T(8,128)}, f32[1,64,128]{2,1,0:T(8,128)S(1)}, u32[]{:S(2)}) copy-start(f32[1,64,128]{2,1,0:T(8,128)S(1)} %collective-permute-done.2) | copy-start | bytes 98308
  35.3 134.3 %copy-start.9 = (f32[1,64,128]{2,1,0:T(8,128)}, f32[1,64,128]{2,1,0:T(8,128)S(1)}, u32[]{:S(2)}) copy-start(f32[1,64,128]{2,1,0:T(8,128)S(1)} %collective-permute-done) | copy-start | bytes 98308
  35.4 11.8 %collective-permute-start.4 = (f32[4,64,1]{2,1,0:T(8,128)S(1)}, f32[4,64,1]{2,1,0:T(8,128)S(1)}, u32[]{:S(2)}, u32[]{:S(2)}) collective-permute-start(f32[4,64,1]{2,1,0:T(8,128)S(1)} %get-tuple-element.37), channel_id=1, source_target_pairs={{0,1},{1,2},{2,3},{3,4},{4,5},{5,6},{6,7},{8,9},{9,10},{10,11},{11... | collective-permute-start | bytes 3080 | tf_op jit(solution)/shard_map/ppermute | solution.py:23
  39.2 8.0 collective-permute-start.6
  41.4 6.9 collective-permute-start.7
  43.3 6.9 collective-permute-start.5
  51.3 17.9 %all-to-all-start = ((f32[2,64,128]{2,0,1:T(2,128)}), f32[2,64,128]{2,0,1:T(2,128)S(1)}, u32[]{:S(2)}, u32[]{:S(2)}) async-start(f32[2,64,128]{2,0,1:T(2,128)} %copy.85), calls=%async_computation | async-start | bytes 131072 | tf_op jit(solution)/shard_map/all_to_all | solution.py:122
  62.4 120.2 %copy-start.25 = (f32[1024]{0:T(1024)}, f32[1024]{0:T(1024)S(1)}, u32[]{:S(2)}) copy-start(f32[1024]{0:T(1024)S(1)} %get-tuple-element.65) | copy-start | bytes 12292
  88.6 11.3 %all-to-all-start.1 = ((f32[32,1,512]{2,1,0:T(1,128)}), f32[32,1,512]{2,1,0:T(1,128)S(1)}, u32[]{:S(2)}, u32[]{:S(2)}) async-start(f32[32,1,512]{2,1,0:T(1,128)} %reshape.171), calls=%async_computation.1 | async-start | bytes 131072 | tf_op jit(solution)/shard_map/all_to_all | solution.py:124
  149.5 4.5 collective-permute-start.9
  152.0 7.3 collective-permute-start.8
  159.4 6.9 collective-permute-start.11
  162.7 6.9 collective-permute-start.10
  216.7 14.1 %all-to-all-start.6 = ((f32[32,1,512]{2,1,0:T(1,128)}), f32[32,1,512]{2,1,0:T(1,128)S(1)}, u32[]{:S(2)}, u32[]{:S(2)}) async-start(f32[32,1,512]{2,1,0:T(1,128)} %reshape.179), calls=%async_computation.6 | async-start | bytes 131072 | tf_op jit(solution)/shard_map/all_to_all | solution.py:132
  221.7 574.5 %collective-permute-start.25 = (f32[8,1,64,128]{3,2,1,0:T(8,128)}, f32[8,1,64,128]{3,2,1,0:T(8,128)}, u32[]{:S(2)}, u32[]{:S(2)}) collective-permute-start(f32[8,1,64,128]{3,2,1,0:T(8,128)} %get-tuple-element.15), channel_id=1, source_target_pairs={{8,0},{16,8},{24,16},{32,24},{40,32},{48,40},{56,48},{64,56},{72,6... | collective-permute-start | bytes 786440 | tf_op jit(solution)/shard_map/ppermute | solution.py:25
  248.8 139.1 %copy-start.8 = (f32[1,64,128]{2,1,0:T(8,128)S(1)}, f32[1,64,128]{2,1,0:T(8,128)}, u32[]{:S(2)}) copy-start(f32[1,64,128]{2,1,0:T(8,128)} %copy-done.7) | copy-start | bytes 98308
  248.8 139.1 %copy-start.10 = (f32[1,64,128]{2,1,0:T(8,128)S(1)}, f32[1,64,128]{2,1,0:T(8,128)}, u32[]{:S(2)}) copy-start(f32[1,64,128]{2,1,0:T(8,128)} %copy-done.9) | copy-start | bytes 98308
  251.6 114.9 %all-to-all-start.7 = ((f32[8,1,2048]{2,1,0:T(1,128)}), f32[8,1,2048]{2,1,0:T(1,128)S(1)}, u32[]{:S(2)}, u32[]{:S(2)}) async-start(f32[8,1,2048]{2,1,0:T(1,128)} %reshape.181), calls=%async_computation.7 | async-start | bytes 131072 | tf_op jit(solution)/shard_map/all_to_all | solution.py:134
  256.3 443.6 %all-reduce.9.cloned.1.call-start = ((), (), s32[]{:S(2)}) async-start(), calls=%async_computation.16 | async-start | bytes 2105344 | tf_op jit(solution)/shard_map/psum | solution.py:140
  369.8 4.4 collective-permute-start.13
  371.7 7.3 collective-permute-start.12
  379.2 6.9 collective-permute-start.15
  381.1 6.9 collective-permute-start.14
  389.1 252.1 %all-to-all-start.8 = ((f32[2,64,128]{2,0,1:T(2,128)}), f32[2,64,128]{2,0,1:T(2,128)S(1)}, u32[]{:S(2)}, u32[]{:S(2)}) async-start(f32[2,64,128]{2,0,1:T(2,128)} %copy.103), calls=%async_computation.8 | async-start | bytes 131072 | tf_op jit(solution)/shard_map/all_to_all | solution.py:122
  661.3 28.2 %all-to-all-start.9 = ((f32[32,1,512]{2,1,0:T(1,128)}), f32[32,1,512]{2,1,0:T(1,128)S(1)}, u32[]{:S(2)}, u32[]{:S(2)}) async-start(f32[32,1,512]{2,1,0:T(1,128)} %reshape.183), calls=%async_computation.9 | async-start | bytes 131072 | tf_op jit(solution)/shard_map/all_to_all | solution.py:124
  694.4 11.4 %all-to-all-start.10 = ((f32[32,1,512]{2,1,0:T(1,128)}), f32[32,1,512]{2,1,0:T(1,128)S(1)}, u32[]{:S(2)}, u32[]{:S(2)}) async-start(f32[32,1,512]{2,1,0:T(1,128)} %reshape.185), calls=%async_computation.10 | async-start | bytes 131072 | tf_op jit(solution)/shard_map/all_to_all | solution.py:132
  699.4 80.1 %all-reduce.11.cloned.1.call-start = ((), (), s32[]{:S(2)}) async-start(), calls=%async_computation.17 | async-start | bytes 2105344 | tf_op jit(solution)/shard_map/psum | solution.py:140
  726.3 62.4 %all-to-all-start.11 = ((f32[8,1,2048]{2,1,0:T(1,128)}), f32[8,1,2048]{2,1,0:T(1,128)S(1)}, u32[]{:S(2)}, u32[]{:S(2)}) async-start(f32[8,1,2048]{2,1,0:T(1,128)} %reshape.187), calls=%async_computation.11 | async-start | bytes 131072 | tf_op jit(solution)/shard_map/all_to_all | solution.py:134
  791.9 5.3 collective-permute-start.17
  793.8 7.3 collective-permute-start.16
  801.9 13.6 %collective-permute-start.19 = (f32[4,64,1]{2,1,0:T(8,128)}, f32[4,64,1]{2,1,0:T(8,128)}, u32[]{:S(2)}, u32[]{:S(2)}) collective-permute-start(f32[4,64,1]{2,1,0:T(8,128)} %get-tuple-element.28), channel_id=1, source_target_pairs={{1,0},{2,1},{3,2},{4,3},{5,4},{6,5},{7,6},{9,8},{10,9},{11,10},{12... | collective-permute-start | bytes 3080 | tf_op jit(solution)/shard_map/ppermute | solution.py:25
  804.7 10.9 %collective-permute-start.18 = (f32[4,64,1]{2,1,0:T(8,128)}, f32[4,64,1]{2,1,0:T(8,128)}, u32[]{:S(2)}, u32[]{:S(2)}) collective-permute-start(f32[4,64,1]{2,1,0:T(8,128)} %get-tuple-element.27), channel_id=1, source_target_pairs={{0,1},{1,2},{2,3},{3,4},{4,5},{5,6},{6,7},{8,9},{9,10},{10,11},{11... | collective-permute-start | bytes 3080 | tf_op jit(solution)/shard_map/ppermute | solution.py:23
  809.2 78.1 %collective-permute-start.27 = (f32[8,4,64,1]{2,0,3,1:T(8,128)}, f32[8,4,64,1]{2,0,3,1:T(8,128)S(1)}, u32[]{:S(2)}, u32[]{:S(2)}) collective-permute-start(f32[8,4,64,1]{2,0,3,1:T(8,128)} %copy.122), channel_id=1, source_target_pairs={{1,0},{2,1},{3,2},{4,3},{5,4},{6,5},{7,6},{9,8},{10,9},{11,10},{12... | collective-permute-start | bytes 24584 | tf_op jit(solution)/shard_map/ppermute | solution.py:25
  813.0 75.7 %collective-permute-start.26 = (f32[8,4,64,1]{2,0,3,1:T(8,128)S(1)}, f32[8,4,64,1]{2,0,3,1:T(8,128)S(1)}, u32[]{:S(2)}, u32[]{:S(2)}) collective-permute-start(f32[8,4,64,1]{2,0,3,1:T(8,128)S(1)} %copy.121), channel_id=1, source_target_pairs={{0,1},{1,2},{2,3},{3,4},{4,5},{5,6},{6,7},{8,9},{9,10},{10,11},{11... | collective-permute-start | bytes 24584 | tf_op jit(solution)/shard_map/ppermute | solution.py:23
  817.6 72.4 %all-to-all-start.12 = ((f32[2,64,128]{2,0,1:T(2,128)}), f32[2,64,128]{2,0,1:T(2,128)S(1)}, u32[]{:S(2)}, u32[]{:S(2)}) async-start(f32[2,64,128]{2,0,1:T(2,128)} %copy.112), calls=%async_computation.12 | async-start | bytes 131072 | tf_op jit(solution)/shard_map/all_to_all | solution.py:122
  909.6 11.6 %all-to-all-start.13 = ((f32[32,1,512]{2,1,0:T(1,128)}), f32[32,1,512]{2,1,0:T(1,128)S(1)}, u32[]{:S(2)}, u32[]{:S(2)}) async-start(f32[32,1,512]{2,1,0:T(1,128)} %reshape.189), calls=%async_computation.13 | async-start | bytes 131072 | tf_op jit(solution)/shard_map/all_to_all | solution.py:124
  926.2 11.4 %all-to-all-start.14 = ((f32[32,1,512]{2,1,0:T(1,128)}), f32[32,1,512]{2,1,0:T(1,128)S(1)}, u32[]{:S(2)}, u32[]{:S(2)}) async-start(f32[32,1,512]{2,1,0:T(1,128)} %reshape.191), calls=%async_computation.14 | async-start | bytes 131072 | tf_op jit(solution)/shard_map/all_to_all | solution.py:132
  958.1 14.1 %all-to-all-start.15 = ((f32[8,1,2048]{2,1,0:T(1,128)}), f32[8,1,2048]{2,1,0:T(1,128)S(1)}, u32[]{:S(2)}, u32[]{:S(2)}) async-start(f32[8,1,2048]{2,1,0:T(1,128)} %reshape.193), calls=%async_computation.15 | async-start | bytes 131072 | tf_op jit(solution)/shard_map/all_to_all | solution.py:134
  977.5 5.4 collective-permute-start.21
  979.7 7.3 collective-permute-start.20
  987.2 6.9 collective-permute-start.23
  990.5 6.9 collective-permute-start.22
  (26 other events, 674.6 us)
Sparse Core Ops, SparseCore 0:
  366.7 114.9 all-reduce.8
  702.6 76.8 all-reduce.10
